TPU v7x, 256 devices: a whole 4x4x8 slice. The times are simulated.
256 devices in a mesh: row: 8 (over y_hi, x), col: 32 (over y_lo, z, core).
Axes of the slice: x: 4, y: 4 (y_hi: 2, y_lo: 2; y = y_hi * 2 + y_lo), z: 8, core: 2. Of those that a mesh axis runs over, the one named last changes fastest.
Arguments:
- features: bfloat16 [131072, 128], P(('col', 'row')), may hold values from -6 to 6
- weight: bfloat16 [128, 256], replicated, may hold values from -0.5 to 0.5
- out_grad: bfloat16 [131072, 256], P(('row', 'col')), may hold values from -0.796875 to 0.796875
- tile_index: int32 [8, 32, 64, 3], P('row', 'col'), may hold values from 0 to 127, as said below
- edge_mask: int32 [8, 32, 64, 128, 128], P('row', 'col'), may hold values 0 or 1
- edge_weight: bfloat16 [8, 32, 64, 128, 128], P('row', 'col'), may hold values from 0 to 1
Outputs:
- edge_grad: bfloat16 [8, 32, 64, 128, 128], P('row', 'col')
- feature_grad: bfloat16 [131072, 128], P(('col', 'row'))
Inputs may be any that keep to these rules, and one draw needn't show every extreme that they name: `tile_index`: within one device the (tile row, tile column) pairs are distinct; tile rows lie below 128, tile columns below 32; live slots come first, a device has between 21 and 64 of them, and some device has all 64 live.
All inputs are finite; a program needn't handle non-finite values. No bound on the sum of `edge_mask` on one device may be relied on, other than what follows from the above.
Results may differ from a plain program's by a relative error of at most 0.0049.
Values may be sent and summed in bfloat16 or wider, within the bound.
A program may use at most 64 MiB of HBM per device.

v0:
```python
import jax
import jax.numpy as jnp
from jax import lax
from jax.sharding import PartitionSpec as P

BLOCK = 128


def local(features, weight, out_grad, tile_index, edge_mask, edge_weight):
    hidden = weight.shape[1]
    grad_rows = lax.all_gather(out_grad, "col", axis=0, tiled=True)
    proj = jnp.dot(features, weight, preferred_element_type=jnp.float32).astype(jnp.bfloat16)
    proj_cols = lax.all_gather(proj, "row", axis=0, tiled=True)
    table = tile_index[0, 0]
    tile_rows = table[:, 0]
    tile_cols = table[:, 1]
    live = table[:, 2].astype(jnp.float32)
    col_blocks = proj_cols.shape[0] // BLOCK
    grad_tiles = jnp.take(grad_rows.reshape(-1, BLOCK, hidden), tile_rows, axis=0)
    proj_tiles = jnp.take(proj_cols.reshape(col_blocks, BLOCK, hidden), tile_cols, axis=0)
    keep = edge_mask[0, 0].astype(jnp.float32) * live[:, None, None]
    scores = jnp.einsum("tif,tjf->tij", grad_tiles, proj_tiles, preferred_element_type=jnp.float32)
    edge_grad = (keep * scores).astype(jnp.bfloat16)[None, None]
    adjacency = (edge_weight[0, 0].astype(jnp.float32) * keep).astype(jnp.bfloat16)
    contrib = jnp.einsum("tij,tif->tjf", adjacency, grad_tiles, preferred_element_type=jnp.float32)
    selector = (tile_cols[:, None] == jnp.arange(col_blocks, dtype=jnp.int32)[None, :]).astype(
        jnp.float32
    )
    partial_grad = jnp.einsum(
        "tc,tjf->cjf", selector, contrib, precision=lax.Precision.HIGHEST
    ).reshape(col_blocks * BLOCK, hidden)
    wide_weight = weight.astype(jnp.float32)
    proj_grad = lax.psum_scatter(partial_grad, "row", scatter_dimension=0, tiled=True)
    feature_grad = jnp.dot(proj_grad, wide_weight.T, precision=lax.Precision.HIGHEST)
    return (edge_grad, feature_grad.astype(jnp.bfloat16))


def solution(mesh):
    in_specs = (
        P(("col", "row"), None),
        P(),
        P(("row", "col"), None),
        P("row", "col", None, None),
        P("row", "col", None, None, None),
        P("row", "col", None, None, None),
    )
    out_specs = (P("row", "col", None, None, None), P(("col", "row"), None))
    return jax.shard_map(local, mesh=mesh, in_specs=in_specs, out_specs=out_specs, check_vma=False)
```

profile of v0, /device:TPU:1, one launch (start us, length us, event | category | flops | bytes accessed | tf_op | source)
XLA Modules:
  0.0 249.8 jit_solution(5098268297364567421)
XLA Ops:
  7.2 0.0 copy-start
  7.2 0.0 all-gather.3.cloned.1.call-start
  7.2 0.7 all-gather.3.cloned.1.call-update
  7.9 0.0 all-gather.5.cloned.1.call-start
  8.0 0.1 copy-done
  8.1 1.7 convolution_convert_fusion
  9.8 0.0 all-gather.5.cloned.1.call-update
  9.8 0.0 reduce-scatter.2.cloned.1.call-start
  9.9 0.7 copy.14
  10.6 75.8 %all-gather.3.cloned.1.call-done = bf16[16384,256]{1,0:T(8,128)(2,1)} async-done(((bf16[512,256]{1,0:T(8,128)(2,1)}), bf16[16384,256]{1,0:T(8,128)(2,1)}) %all-gather.3.cloned.1.call-update) | async-done | bytes 8388624 | tf_op jit(solution)/shard_map/all_gather | solution.py:11
  86.4 0.0 copy-start.1
  86.4 6.3 %gather_fusion = bf16[64,128,256]{2,1,0:T(8,128)(2,1)} fusion(bf16[128,128,256]{2,1,0:T(8,128)(2,1)} %bitcast.44, s32[1024]{0:T(1024)S(1)} %get-tuple-element.9), kind=kCustom, calls=%fused_computation | custom fusion | bytes 8388864 | tf_op jit(solution)/shard_map/jit(_take)/gather | solution.py:19
  92.7 0.0 copy-done.1
  92.7 5.1 %fusion.7 = f32[64,128,256]{2,1,0:T(8,128)S(1)} fusion(s32[1,1,64,128,128]{4,3,2,1,0:T(8,128)} %param.10, bf16[1,1,64,128,128]{4,3,2,1,0:T(8,128)(2,1)S(1)} %copy-done.1, f32[64]{0:T(128)S(1)} %get-tuple-element.5, bf16[64,128,256]{2,1,0:T(8,128)(2,1)} %gather_fusion, pred[64]{0:T(512)(128)(4,1)S(1)} %get-tuple-element.6), kind=kOutput, calls=%fused_computation.13 | convolution fusion | flops 544210944 | bytes 18874688 | tf_op jit(solution)/shard_map/tij,tif->tjf/dot_general | solution.py:25
  97.8 8.3 %fusion = f32[32,128,256]{2,0,1:T(8,128)S(1)} fusion(f32[64,128,256]{2,1,0:T(8,128)S(1)} %fusion.7, s32[64]{0:T(128)S(1)} %get-tuple-element.2), kind=kOutput, calls=%fused_computation.2 | convolution fusion | flops 805308416 | bytes 12583168 | tf_op jit(solution)/shard_map/tc,tjf->cjf/dot_general | solution.py:29
  106.2 4.6 %copy.8 = f32[32,128,256]{2,1,0:T(8,128)} copy(f32[32,128,256]{2,0,1:T(8,128)S(1)} %fusion) | data formatting | bytes 8388608 | tf_op jit(solution)/shard_map/tc,tjf->cjf/dot_general | solution.py:29
  110.7 0.0 reduce-scatter.2.cloned.1.call-update
  110.8 37.1 %all-gather.5.cloned.1.call-done = bf16[4096,256]{1,0:T(8,128)(2,1)} async-done(((bf16[512,256]{1,0:T(8,128)(2,1)}), bf16[4096,256]{1,0:T(8,128)(2,1)}) %all-gather.5.cloned.1.call-update) | async-done | bytes 2097168 | tf_op jit(solution)/shard_map/all_gather | solution.py:13
  147.8 4.4 %gather_fusion.1 = bf16[64,128,256]{2,1,0:T(8,128)(2,1)} fusion(bf16[32,128,256]{2,1,0:T(8,128)(2,1)} %bitcast.43, s32[1024]{0:T(1024)S(1)} %get-tuple-element.8), kind=kCustom, calls=%fused_computation.1 | custom fusion | bytes 8388864 | tf_op jit(solution)/shard_map/jit(_take)/gather | solution.py:20
  152.2 0.0 copy-start.2
  152.2 7.5 %fusion.6 = bf16[1,1,64,128,128]{4,3,2,1,0:T(8,128)(2,1)} fusion(s32[1,1,64,128,128]{4,3,2,1,0:T(8,128)} %param.10, f32[64]{0:T(128)S(1)} %get-tuple-element.5, bf16[64,128,256]{2,1,0:T(8,128)(2,1)} %gather_fusion.1, pred[64]{0:T(512)(128)(4,1)S(1)} %get-tuple-element.7, bf16[64,128,256]{2,1,0:T(8,128)(2,1)} %gather_fusion, ...), kind=kOutput, calls=%fused_computation.12 | convolution fusion | flops 545259520 | bytes 14680448 | tf_op jit(solution)/shard_map/tif,tjf->tij/dot_general | solution.py:22
  159.7 81.5 %reduce-scatter.2.cloned.1.call-done = f32[512,256]{1,0:T(8,128)} async-done(((f32[4096,256]{1,0:T(8,128)}), f32[512,256]{1,0:T(8,128)}) %reduce-scatter.2.cloned.1.call-update) | async-done | bytes 524304 | tf_op jit(solution)/shard_map/reduce_scatter | solution.py:33
  241.2 0.0 copy-done.2
  241.2 2.1 convolution_convert_fusion.1
  (3 shorter events, 0.0 us)
Async XLA Ops:
  7.2 0.9 copy-start
  7.2 79.2 %all-gather.3.cloned.1.call-start = ((), (), s32[]{:S(2)}) async-start(), calls=%async_computation.1 | async-start | bytes 8650752 | tf_op jit(solution)/shard_map/all_gather | solution.py:11
  7.9 139.9 %all-gather.5.cloned.1.call-start = ((), (), s32[]{:S(2)}) async-start(), calls=%async_computation.2 | async-start | bytes 2359296 | tf_op jit(solution)/shard_map/all_gather | solution.py:13
  9.8 231.3 %reduce-scatter.2.cloned.1.call-start = ((), (), s32[]{:S(2)}) async-start(), calls=%async_computation.3 | async-start | bytes 4718592 | tf_op jit(solution)/shard_map/reduce_scatter | solution.py:33
  86.4 6.3 %copy-start.1 = (bf16[1,1,64,128,128]{4,3,2,1,0:T(8,128)(2,1)S(1)}, bf16[1,1,64,128,128]{4,3,2,1,0:T(8,128)(2,1)}, u32[]{:S(2)}) copy-start(bf16[1,1,64,128,128]{4,3,2,1,0:T(8,128)(2,1)} %param.11) | copy-start | bytes 6291460
  152.2 89.0 %copy-start.2 = (bf16[128,256]{1,0:T(8,128)(2,1)S(1)}, bf16[128,256]{1,0:T(8,128)(2,1)}, u32[]{:S(2)}) copy-start(bf16[128,256]{1,0:T(8,128)(2,1)} %param.7) | copy-start | bytes 196612
Sparse Core Ops, SparseCore 0:
  9.9 76.4 all-gather.2
  89.6 58.1 all-gather.4
  152.0 89.1 reduce-scatter.1
where the time goes:
time: 250 us
  waiting for transfers between devices  195 us (78%)
  matrix products  24.8 us (10%)
  local copies, waits for them, and re-layouts  16 us (6%)
  between operations  13.8 us (6%)
    reduce_scatter x1, waiting for transfers between devices, local(): lax.psum_scatter(partial_grad, 'row', scatter_dimension=0, tiled=True)  81.5 us
    all_gather x1, waiting for transfers between devices, local(): grad_rows = lax.all_gather(out_grad, 'col', axis=0, tiled=True)  75.8 us
    all_gather x1, waiting for transfers between devices, local(): proj_cols = lax.all_gather(proj, 'row', axis=0, tiled=True)  37.1 us
    dot_general x1, matrix products, local(): jnp.einsum('tc,tjf->cjf', selector, contrib, precision=lax.Precision.HIGH...  8.32 us
    dot_general x1, matrix products, local(): jnp.einsum('tif,tjf->tij', grad_tiles, proj_tiles, preferred_element_type...  7.51 us
    gather x1, local copies, waits for them, and re-layouts, local(): jnp.take(grad_rows.reshape(-1, BLOCK, hidden), tile_rows, axis=0)  6.3 us
    dot_general x1, matrix products, local(): jnp.einsum('tij,tif->tjf', adjacency, grad_tiles, preferred_element_type=...  5.12 us
  transfers between devices with their start and end apart: 3, of which 3 were waited for; matrix products, arithmetic and copies ran while one was open for 15% of the time, Pallas kernels for 0%

commit v1 on v0

v1 whole, which is shorter than its diff:
```python
import jax
import jax.numpy as jnp
from jax import lax
from jax.experimental import pallas as pl
from jax.experimental.pallas import tpu as pltpu
from jax.sharding import PartitionSpec as P

BLOCK = 128
STEP = 8


def tiles_kernel(table, grads, feats, mask, weight, edge_grad, partial):
    step = pl.program_id(0)

    @pl.when(step == 0)
    def _():
        partial[...] = jnp.zeros_like(partial)

    for k in range(STEP):
        slot = step * STEP + k
        row, col, live = table[3 * slot], table[3 * slot + 1], table[3 * slot + 2]
        keep = mask[k] * live != 0
        rows = grads[row]
        scores = lax.dot_general(
            rows, feats[col], (((1,), (1,)), ((), ())), preferred_element_type=jnp.float32
        )
        edge_grad[k] = jnp.where(keep, scores, 0.0).astype(jnp.bfloat16)
        adjacency = jnp.where(keep, weight[k].astype(jnp.float32), 0.0).astype(jnp.bfloat16)
        partial[col] += lax.dot_general(
            adjacency, rows, (((0,), (0,)), ((), ())), preferred_element_type=jnp.float32
        )


def tiles(table, grads, feats, mask, weight):
    slots, width = mask.shape[0], grads.shape[-1]
    whole = lambda a: pl.BlockSpec(a.shape, lambda i, t: (0, 0, 0), pipeline_mode=pl.Buffered(1))
    some = pl.BlockSpec((STEP, BLOCK, BLOCK), lambda i, t: (i, 0, 0))
    out = jax.ShapeDtypeStruct(feats.shape, jnp.float32)
    return pl.pallas_call(
        tiles_kernel,
        grid_spec=pltpu.PrefetchScalarGridSpec(
            num_scalar_prefetch=1,
            grid=(slots // STEP,),
            in_specs=[whole(grads), whole(feats), some, some],
            out_specs=[some, pl.BlockSpec(out.shape, lambda i, t: (0, 0, 0))],
        ),
        out_shape=[jax.ShapeDtypeStruct(mask.shape, jnp.bfloat16), out],
        compiler_params=pltpu.CompilerParams(vmem_limit_bytes=32 << 20),
    )(table.reshape(-1), grads, feats, mask, weight)


def local(features, weight, out_grad, tile_index, edge_mask, edge_weight):
    width = features.shape[1]
    folded = lax.dot_general(
        out_grad, weight, (((1,), (1,)), ((), ())), preferred_element_type=jnp.float32
    ).astype(jnp.bfloat16)
    grads = lax.all_gather(folded, "col", axis=0, tiled=True).reshape(-1, BLOCK, width)
    feats = lax.all_gather(features, "row", axis=0, tiled=True).reshape(-1, BLOCK, width)
    edge_grad, partial = tiles(tile_index[0, 0], grads, feats, edge_mask[0, 0], edge_weight[0, 0])
    feature_grad = lax.psum_scatter(
        partial.reshape(-1, width), "row", scatter_dimension=0, tiled=True
    )
    return (edge_grad[None, None], feature_grad.astype(jnp.bfloat16))


def solution(mesh):
    in_specs = (
        P(("col", "row"), None),
        P(),
        P(("row", "col"), None),
        P("row", "col", None, None),
        P("row", "col", None, None, None),
        P("row", "col", None, None, None),
    )
    out_specs = (P("row", "col", None, None, None), P(("col", "row"), None))
    return jax.shard_map(local, mesh=mesh, in_specs=in_specs, out_specs=out_specs, check_vma=False)
```

time: 250 us -> 236 us (0.944)
  matrix products: 24.8 us -> 1.72 us
  waiting for transfers between devices: 195 us -> 204 us
  local copies, waits for them, and re-layouts: 16 us -> 8.26 us
  Pallas kernels: 0 us -> 6.45 us
    dot_general x5 -> x1, matrix products: 24.8 us -> 1.72 us  [local(): lax.dot_general(out_grad, weight, (((1,), (1,)), ((), ())), preferred_ele...]
    all_gather x2, waiting for transfers between devices: 113 us -> 125 us  [the longest x1 69.5 us: local(): lax.all_gather(folded, 'col', axis=0, tiled=True).reshape(-1, BLOCK, width)]
    gather x2 -> x0, local copies, waits for them, and re-layouts: 10.7 us -> none  [the longest x1 6.3 us: local(): jnp.take(grad_rows.reshape(-1, BLOCK, hidden), tile_rows, axis=0)]
    unnamed x7 -> x11, local copies, waits for them, and re-layouts: 0.81 us -> 8.13 us
    pallas_call x0 -> x1, Pallas kernels: none -> 6.45 us  [tiles(): pl.pallas_call(tiles_kernel, grid_spec=pltpu.PrefetchScalarGridSpec(num_s...]
    dot_general x1 -> x0, local copies, waits for them, and re-layouts: 4.56 us -> none  [local(): jnp.einsum('tc,tjf->cjf', selector, contrib, precision=lax.Precision.HIGH...]
    reduce_scatter x1, waiting for transfers between devices: 81.5 us -> 78.4 us  [local(): lax.psum_scatter(partial.reshape(-1, width), 'row', scatter_dimension=0,...]
  transfers between devices with their start and end apart: 3 -> 3, of which waited for: 3 -> 3; matrix products, arithmetic and copies ran while one was open for 15% -> 1% of each run, Pallas kernels for 0% -> 0%
where the time goes in v1:
time: 236 us
  waiting for transfers between devices  204 us (86%)
  between operations  13.8 us (6%)
  local copies, waits for them, and re-layouts  8.26 us (4%)
  Pallas kernels  6.45 us (3%)
    reduce_scatter x1, waiting for transfers between devices, local(): lax.psum_scatter(partial.reshape(-1, width), 'row', scatter_dimension=0,...  78.4 us
    all_gather x1, waiting for transfers between devices, local(): lax.all_gather(folded, 'col', axis=0, tiled=True).reshape(-1, BLOCK, width)  69.5 us
    all_gather x1, waiting for transfers between devices, local(): lax.all_gather(features, 'row', axis=0, tiled=True)  55.2 us
    unnamed x11, local copies, waits for them, and re-layouts  8.13 us
    pallas_call x1, Pallas kernels, tiles(): pl.pallas_call(tiles_kernel, grid_spec=pltpu.PrefetchScalarGridSpec(num_s...  6.45 us
  transfers between devices with their start and end apart: 3, of which 3 were waited for; matrix products, arithmetic and copies ran while one was open for 1% of the time, Pallas kernels for 0%

profile of v1, /device:TPU:1, one launch (start us, length us, event | category | flops | bytes accessed | tf_op | source)
XLA Modules:
  0.0 235.7 jit_solution(525745734567490981)
XLA Ops:
  7.2 0.0 copy-start
  7.2 0.0 all-gather.5.cloned.1.call-start
  7.2 0.7 all-gather.5.cloned.1.call-update
  7.9 0.0 all-gather.3.cloned.1.call-start
  8.0 0.2 copy-done
  8.1 1.7 convolution_convert_fusion
  9.8 0.0 all-gather.3.cloned.1.call-update
  9.9 0.0 reduce-scatter.2.cloned.1.call-start
  9.9 0.8 copy.8
  10.7 0.1 reshape_squeeze.3.table
  10.8 55.2 %all-gather.5.cloned.1.call-done = bf16[4096,128]{1,0:T(8,128)(2,1)} async-done(((bf16[512,128]{1,0:T(8,128)(2,1)}), bf16[4096,128]{1,0:T(8,128)(2,1)}) %all-gather.5.cloned.1.call-update) | async-done | bytes 1048592 | tf_op jit(solution)/shard_map/all_gather | solution.py:58
  66.0 69.5 %all-gather.3.cloned.1.call-done = bf16[16384,128]{1,0:T(8,128)(2,1)} async-done(((bf16[512,128]{1,0:T(8,128)(2,1)}), bf16[16384,128]{1,0:T(8,128)(2,1)}) %all-gather.3.cloned.1.call-update) | async-done | bytes 4194320 | tf_op jit(solution)/shard_map/all_gather | solution.py:57
  135.5 0.0 copy-start.1
  135.5 2.2 copy-done.1
  137.7 0.0 copy-start.2
  137.7 2.2 copy-done.2
  139.9 0.0 copy-start.3
  139.9 1.6 copy-done.3
  141.5 0.0 copy-start.4
  141.5 1.2 copy-done.4
  142.7 6.4 %shard_map.77 = (bf16[64,128,128]{2,1,0:T(8,128)(2,1)}, f32[32,128,128]{2,1,0:T(8,128)}) custom-call(s32[192]{0:T(256)S(1)} %reshape_squeeze.3.table, bf16[128,128,128]{2,1,0:T(8,128)(2,1)S(1)} %bitcast.11, bf16[32,128,128]{2,1,0:T(8,128)(2,1)S(1)} %bitcast.13, s32[64,128,128]{2,1,0:T(8,128)S(1)} %bitcast.10, bf16[64,128,128]{2,1,0:T(8,128)(2,1)S(1)} %bitcast.12), custom_call_target="tpu_custom_call" | custom-call | tf_op jit(solution)/shard_map/pallas_call | solution.py:39
  149.2 0.0 reduce-scatter.2.cloned.1.call-update
  149.2 78.4 %reduce-scatter.2.cloned.1.call-done = f32[512,128]{1,0:T(8,128)} async-done(((f32[4096,128]{1,0:T(8,128)}), f32[512,128]{1,0:T(8,128)}) %reduce-scatter.2.cloned.1.call-update) | async-done | bytes 262160 | tf_op jit(solution)/shard_map/reduce_scatter | solution.py:60
  227.6 1.6 convert_element_type.7
Async XLA Ops:
  7.2 1.0 copy-start
  7.2 58.8 %all-gather.5.cloned.1.call-start = ((), (), s32[]{:S(2)}) async-start(), calls=%async_computation.2 | async-start | bytes 1179648 | tf_op jit(solution)/shard_map/all_gather | solution.py:58
  7.9 127.6 %all-gather.3.cloned.1.call-start = ((), (), s32[]{:S(2)}) async-start(), calls=%async_computation.1 | async-start | bytes 4325376 | tf_op jit(solution)/shard_map/all_gather | solution.py:57
  9.9 217.7 %reduce-scatter.2.cloned.1.call-start = ((), (), s32[]{:S(2)}) async-start(), calls=%async_computation.3 | async-start | bytes 2359296 | tf_op jit(solution)/shard_map/reduce_scatter | solution.py:60
  135.5 2.2 copy-start.1
  137.7 2.2 copy-start.2
  139.9 1.6 copy-start.3
  141.5 1.2 copy-start.4
Sparse Core Ops, SparseCore 0:
  10.6 55.3 all-gather.4
  68.4 67.0 all-gather.2
  149.3 78.2 reduce-scatter.1

commit v2 on v0

v2 whole, which is shorter than its diff:
```python
import jax
import jax.numpy as jnp
from jax import lax
from jax.experimental import pallas as pl
from jax.experimental.pallas import tpu as pltpu
from jax.sharding import PartitionSpec as P

MESH = pl.DeviceIdType.MESH
BLOCK = 128
NX, NZ = 4, 8
CHUNK = 8
F32, BF16 = jnp.float32, jnp.bfloat16


def kernel(
    table,
    table_v,
    out_grad,
    weight,
    features,
    edge_mask,
    edge_weight,
    edge_grad,
    feature_grad,
    hbuf,
    xbuf,
    mask,
    wts,
    adj,
    sums,
    edge_out,
    stage,
    merged,
    relayed,
    landed,
    chain_v,
    chain,
    load_sem,
    out_sem,
    h_send,
    h_recv,
    x_send,
    x_recv,
    g_send,
    g_recv,
):
    slots = mask.shape[0]
    r, c = lax.axis_index("row"), lax.axis_index("col")
    yh, x = r // NX, r % NX
    yl, z, k = c // (2 * NZ), (c // 2) % NZ, c % 2

    def col_of(yl, z, k):
        return (yl * NZ + (z + NZ) % NZ) * 2 + k

    def row_of(yh, x):
        return yh * NX + (x + NX) % NX

    to_z = {s: (r, col_of(yl, z + s, k)) for s in (1, -1)}
    to_y = (r, col_of(1 - yl, z, k))
    to_core = (r, col_of(yl, z, 1 - k))
    to_row = {
        (q, s): (row_of((yh + q) % 2, x + s), c)
        for q in (0, 1)
        for s in (-1, 0, 1)
        if q or s
    }

    loads = [
        pltpu.make_async_copy(features, xbuf.at[pl.ds(4 * r, 4)], load_sem.at[0]),
        pltpu.make_async_copy(edge_mask, mask, load_sem.at[1]),
        pltpu.make_async_copy(edge_weight, wts, load_sem.at[2]),
    ]
    for load in loads:
        load.start()

    barrier = pltpu.get_barrier_semaphore()
    peers = [to_z[1], to_z[-1], to_y, to_core, *to_row.values()]
    for peer in peers:
        pl.semaphore_signal(barrier, inc=1, device_id=peer, device_id_type=MESH)

    folded = lax.dot_general(
        out_grad[...], weight[...], (((1,), (1,)), ((), ())), preferred_element_type=F32
    ).astype(BF16)
    for b in range(4):
        hbuf[4 * c + b] = folded[b * BLOCK : (b + 1) * BLOCK]
    pl.semaphore_wait(barrier, len(peers))

    started = []

    def h_copy(block, half, device, i):
        piece = hbuf.at[pl.ds(4 * block + 2 * half, 2)]
        return pltpu.make_async_remote_copy(
            src_ref=piece,
            dst_ref=piece,
            send_sem=h_send.at[i],
            recv_sem=h_recv.at[2 * block + half],
            device_id=device,
            device_id_type=MESH,
        )

    def put(block, half, device):
        copy = h_copy(block, half, device, len(started))
        copy.start()
        started.append(copy)

    def got(block, half):
        h_copy(block, half, to_core, 0).wait_recv()

    x_started = []

    def x_copy(block, part, n, device, i, sem):
        piece = xbuf.at[pl.ds(4 * block + part, n)]
        return pltpu.make_async_remote_copy(
            src_ref=piece,
            dst_ref=piece,
            send_sem=x_send.at[i],
            recv_sem=x_recv.at[sem],
            device_id=device,
            device_id_type=MESH,
        )

    def x_put(block, part, n, device, sem):
        copy = x_copy(block, part, n, device, len(x_started), sem)
        copy.start()
        x_started.append(copy)

    def x_got(block, part, n, sem):
        x_copy(block, part, n, to_core, 0, sem).wait_recv()

    put(c, 0, to_y)
    put(c, 0, to_z[1])
    put(c, 0, to_z[-1])
    put(c, 1, to_z[1])
    put(c, 1, to_z[-1])
    put(c, 1, to_y)
    put(c, 0, to_core)
    put(c, 1, to_core)
    loads[0].wait()
    x_put(r, 0, 4, to_row[0, 1], 1)
    x_put(r, 0, 4, to_row[0, -1], 2)
    x_put(r, 0, 4, to_row[1, 0], 0)

    cols = table_v[1:2, :]
    wide = jnp.broadcast_to(cols, (slots, slots))
    at_s = lax.broadcasted_iota(jnp.int32, (slots, slots), 0)
    at_q = lax.broadcasted_iota(jnp.int32, (slots, slots), 1)
    tall = jnp.sum(jnp.where(at_s == at_q, wide, 0), axis=1, keepdims=True)
    chain_v[0:1, 0:slots] = jnp.max(
        jnp.where((tall == wide) & (at_s < at_q), at_s, -1), axis=0, keepdims=True
    )
    chain_v[1:2, 0:slots] = jnp.max(jnp.where(tall == at_q, at_s, -1), axis=0, keepdims=True)
    to_scalar = pltpu.make_async_copy(chain_v, chain, load_sem.at[3])
    to_scalar.start()

    loads[1].wait()
    loads[2].wait()

    def prepare(first, n):
        def one(t, carry):
            keep = mask[t] * table[2, t] != 0
            kept = jnp.where(keep, wts[t].astype(F32), 0.0)
            adj[t] = kept.T.astype(BF16)
            return carry

        lax.fori_loop(first, first + n, one, 0, unroll=2)

    mate = col_of(1 - yl, z, k)
    got(mate, 0)
    put(mate, 0, to_z[1])
    put(mate, 0, to_z[-1])
    put(mate, 0, to_core)
    prepare(0, 8)

    done = 8
    for s in range(1, 4):
        for sign in (1, -1):
            near = col_of(yl, z - sign * s, k)
            far = col_of(1 - yl, z - sign * s, k)
            for half in (0, 1):
                got(near, half)
                if s < 3 or half == (0 if sign > 0 else 1):
                    put(near, half, to_z[sign])
                if half:
                    put(near, half, to_y)
                put(near, half, to_core)
            got(far, 0)
            if s < 3:
                put(far, 0, to_z[sign])
            put(far, 0, to_core)
        if s == 3:
            way = 1 - 2 * k
            put(col_of(1 - yl, z - 3 * way, k), 0, (r, col_of(yl, z + way, k)))
        for back in (s - 1,) if s == 1 else (s - 1, 1 - s):
            late = col_of(1 - yl, z + back, k)
            got(late, 1)
            put(late, 1, to_core)
        if s == 1:
            other = row_of(1 - yh, x)
            x_got(other, 0, 4, 0)
            x_put(other, 0, 4, to_row[0, 1], 3)
            x_put(other, 0, 4, to_row[0, -1], 4)
        if s == 2:
            left, right = row_of(yh, x - 1), row_of(yh, x + 1)
            x_got(left, 0, 4, 1)
            x_put(left, 0, 2, to_row[0, 1], 5)
            x_got(right, 0, 4, 2)
            x_put(right, 2, 2, to_row[0, -1], 6)
        if s == 3:
            left, right = row_of(1 - yh, x - 1), row_of(1 - yh, x + 1)
            x_got(left, 0, 4, 3)
            x_put(left, 0, 2, to_row[0, 1], 7)
            x_got(right, 0, 4, 4)
            x_put(right, 2, 2, to_row[0, -1], 8)
        more = 24 if s < 3 else slots - done
        if more:
            prepare(done, more)
        done += more
    near, far = col_of(yl, z + 4, k), col_of(1 - yl, z + 4, k)
    got(near, 1)
    put(near, 1, to_y)
    put(near, 1, to_core)
    got(near, 0)
    put(near, 0, to_core)
    got(far, 0)
    put(far, 0, to_core)
    for s in (3, -3, 4):
        late = col_of(1 - yl, z + s, k)
        got(late, 1)
        put(late, 1, to_core)

    def from_core(i, carry):
        got(2 * i + 1 - k, 0)
        got(2 * i + 1 - k, 1)
        return carry

    lax.fori_loop(0, 2 * NZ, from_core, 0)
    to_scalar.wait()

    def add(t, carry):
        before = chain[0, t]
        part = jnp.dot(adj[t], hbuf[table[0, t]], preferred_element_type=F32)
        sums[t] = part + jnp.where(before >= 0, sums[jnp.maximum(before, 0)], 0.0)
        return carry

    lax.fori_loop(0, slots, add, 0, unroll=4)

    def total(block):
        final = chain[1, block]
        return jnp.where(final >= 0, sums[jnp.maximum(final, 0)], 0.0)

    def fill(dest, first, n):
        for b in range(first, first + n):
            stage[4 * dest + b] = total(4 * dest + b).astype(BF16)

    g_started = []

    def g_put(src, dst, sem, device):
        copy = pltpu.make_async_remote_copy(
            src_ref=src,
            dst_ref=dst,
            send_sem=g_send.at[len(g_started)],
            recv_sem=g_recv.at[sem],
            device_id=device,
            device_id_type=MESH,
        )
        copy.start()
        g_started.append(copy)

    def g_got(dst, sem):
        pltpu.make_async_remote_copy(
            src_ref=dst,
            dst_ref=dst,
            send_sem=g_send.at[0],
            recv_sem=g_recv.at[sem],
            device_id=to_core,
            device_id_type=MESH,
        ).wait_recv()

    sides = ((1, 0), (-1, 1))
    for q in (0, 1):
        dest = row_of((yh + q) % 2, x + 2)
        fill(dest, 0, 4)
        for s, half in sides:
            i = 2 * q + half
            g_put(
                stage.at[pl.ds(4 * dest + 2 * half, 2)],
                relayed.at[pl.ds(2 * i, 2)],
                i,
                to_row[0, s],
            )
    for q in (1, 0):
        for s, half in sides:
            dest = row_of((yh + q) % 2, x + s)
            fill(dest, 0, 4)
            i = 2 * q + half
            plain = 1 - half
            g_put(
                stage.at[pl.ds(4 * dest + 2 * plain, 2)],
                landed.at[pl.ds(4 * i + 2 * plain, 2)],
                4 + 2 * i + plain,
                to_row[q, s],
            )
    dest = row_of(1 - yh, x)
    fill(dest, 0, 4)
    g_put(stage.at[pl.ds(4 * dest, 4)], landed.at[pl.ds(16, 4)], 12, to_row[1, 0])
    for q in (1, 0):
        for s, half in sides:
            dest = row_of((yh + q) % 2, x + s)
            i = 2 * q + half
            g_got(relayed.at[pl.ds(2 * i, 2)], i)
            for b in (0, 1):
                merged[2 * i + b] = (
                    total(4 * dest + 2 * half + b) + relayed[2 * i + b].astype(F32)
                ).astype(BF16)
            g_put(
                merged.at[pl.ds(2 * i, 2)],
                landed.at[pl.ds(4 * i + 2 * half, 2)],
                4 + 2 * i + half,
                to_row[q, s],
            )

    far_x = row_of(yh, x + 2)
    x_got(far_x, 0, 2, 5)
    x_got(far_x, 2, 2, 6)
    far_x = row_of(1 - yh, x + 2)
    x_got(far_x, 0, 2, 7)
    x_got(far_x, 2, 2, 8)

    def chunk_out(i):
        part = pl.ds(i * CHUNK, CHUNK)
        return pltpu.make_async_copy(edge_out.at[part], edge_grad.at[part], out_sem.at[i])

    def chunk(i, carry):
        for j in range(CHUNK):
            t = i * CHUNK + j
            keep = mask[t] * table[2, t] != 0
            scores = lax.dot_general(
                hbuf[table[0, t]],
                xbuf[table[1, t]],
                (((1,), (1,)), ((), ())),
                preferred_element_type=F32,
            )
            edge_out[t] = jnp.where(keep, scores, 0.0).astype(BF16)
        chunk_out(i).start()
        return carry

    lax.fori_loop(0, slots // CHUNK, chunk, 0)

    for i in range(4):
        for half in (0, 1):
            g_got(landed.at[pl.ds(4 * i + 2 * half, 2)], 4 + 2 * i + half)
    g_got(landed.at[pl.ds(16, 4)], 12)
    for b in range(4):
        value = total(4 * r + b)
        for i in range(5):
            value += landed[4 * i + b].astype(F32)
        feature_grad[b] = value.astype(BF16)

    for copy in started + x_started + g_started:
        copy.wait_send()
    for i in range(slots // CHUNK):
        chunk_out(i).wait()


def local(features, weight, out_grad, tile_index, edge_mask, edge_weight):
    nodes, width = features.shape
    slots = edge_mask.shape[2]
    table = tile_index[0, 0].T
    blocks = nodes // BLOCK
    vmem = pl.BlockSpec(memory_space=pltpu.VMEM)
    hbm = pl.BlockSpec(memory_space=pl.ANY)
    dma = pltpu.SemaphoreType.DMA
    tile = (BLOCK, BLOCK)
    edge_grad, feature_grad = pl.pallas_call(
        kernel,
        in_specs=[pl.BlockSpec(memory_space=pltpu.SMEM), vmem, vmem, vmem, hbm, hbm, hbm],
        out_specs=[hbm, vmem],
        out_shape=[
            jax.ShapeDtypeStruct((slots, *tile), BF16),
            jax.ShapeDtypeStruct((blocks, *tile), BF16),
        ],
        scratch_shapes=[
            pltpu.VMEM((4 * blocks * NZ, *tile), BF16),
            pltpu.VMEM((2 * blocks * NX, *tile), BF16),
            pltpu.VMEM((slots, *tile), jnp.int32),
            pltpu.VMEM((slots, *tile), BF16),
            pltpu.VMEM((slots, *tile), BF16),
            pltpu.VMEM((slots, *tile), F32),
            pltpu.VMEM((slots, *tile), BF16),
            pltpu.VMEM((2 * blocks * NX, *tile), BF16),
            pltpu.VMEM((8, *tile), BF16),
            pltpu.VMEM((8, *tile), BF16),
            pltpu.VMEM((20, *tile), BF16),
            pltpu.VMEM((8, 128), jnp.int32),
            pltpu.SMEM((8, 128), jnp.int32),
            dma((4,)),
            dma((slots // CHUNK,)),
            dma((62,)),
            dma((64,)),
            dma((9,)),
            dma((9,)),
            dma((13,)),
            dma((13,)),
        ],
        compiler_params=pltpu.CompilerParams(
            collective_id=0, has_side_effects=True, vmem_limit_bytes=56 << 20
        ),
        name="layer",
    )(
        table,
        table,
        out_grad,
        weight,
        features.reshape(blocks, *tile),
        edge_mask[0, 0],
        edge_weight[0, 0],
    )
    return (edge_grad[None, None], feature_grad.reshape(nodes, width))


def solution(mesh):
    in_specs = (
        P(("col", "row"), None),
        P(),
        P(("row", "col"), None),
        P("row", "col", None, None),
        P("row", "col", None, None, None),
        P("row", "col", None, None, None),
    )
    out_specs = (P("row", "col", None, None, None), P(("col", "row"), None))
    return jax.shard_map(local, mesh=mesh, in_specs=in_specs, out_specs=out_specs, check_vma=False)
```

time: 250 us -> 57.9 us (0.23)
  waiting for transfers between devices: 195 us -> 0 us
  Pallas kernels: 0 us -> 52 us
  matrix products: 24.8 us -> 0 us
  between operations: 13.8 us -> 0.65 us
  local copies, waits for them, and re-layouts: 16 us -> 5.11 us
    all_gather x2 -> x0, waiting for transfers between devices: 113 us -> none  [the longest x1 75.8 us: local(): grad_rows = lax.all_gather(out_grad, 'col', axis=0, tiled=True)]
    reduce_scatter x1 -> x0, waiting for transfers between devices: 81.5 us -> none  [local(): lax.psum_scatter(partial_grad, 'row', scatter_dimension=0, tiled=True)]
    pallas_call x0 -> x1, Pallas kernels: none -> 52 us  [local(): pl.pallas_call(kernel, in_specs=[pl.BlockSpec(memory_space=pltpu.SMEM), v...]
    dot_general x5 -> x0, matrix products: 24.8 us -> none  [the longest x1 8.32 us: local(): jnp.einsum('tc,tjf->cjf', selector, contrib, precision=lax.Precision.HIGH...]
    gather x2 -> x0, local copies, waits for them, and re-layouts: 10.7 us -> none  [the longest x1 6.3 us: local(): jnp.take(grad_rows.reshape(-1, BLOCK, hidden), tile_rows, axis=0)]
    dot_general x1 -> x0, local copies, waits for them, and re-layouts: 4.56 us -> none  [local(): jnp.einsum('tc,tjf->cjf', selector, contrib, precision=lax.Precision.HIGH...]
    unnamed x7 -> x5, local copies, waits for them, and re-layouts: 0.81 us -> 5.11 us
  transfers between devices with their start and end apart: 3 -> 0, of which waited for: 3 -> 0; matrix products, arithmetic and copies ran while one was open for 15% -> 0% of each run, Pallas kernels for 0% -> 0%
where the time goes in v2:
time: 57.9 us; the launch traced here: 57.8 us
  Pallas kernels  52 us (90%)
  local copies, waits for them, and re-layouts  5.11 us (9%)
  between operations  0.65 us (1%)
    pallas_call x1, Pallas kernels, local(): pl.pallas_call(kernel, in_specs=[pl.BlockSpec(memory_space=pltpu.SMEM), v...  52 us
    unnamed x5, local copies, waits for them, and re-layouts  5.11 us

profile of v2, /device:TPU:1, one launch (start us, length us, event | category | flops | bytes accessed | tf_op | source)
XLA Modules:
  0.0 57.8 jit_solution(6024829442549836318)
XLA Ops:
  0.6 1.3 %copy.10 = s32[1,1,64,3]{2,3,1,0:T(4,128)} copy(s32[1,1,64,3]{2,1,3,0:T(1,128)} %param.9) | data formatting | bytes 1536
  1.9 52.0 %layer.1 = (bf16[64,128,128]{2,1,0:T(8,128)(2,1)}, bf16[4,128,128]{2,1,0:T(8,128)(2,1)}) custom-call(s32[3,64]{1,0:T(4,128)} %bitcast.15, s32[3,64]{1,0:T(4,128)} %bitcast.16, bf16[512,256]{1,0:T(8,128)(2,1)} %out_grad.1, bf16[128,256]{1,0:T(8,128)(2,1)} %weight.1, bf16[4,128,128]{2,1,0:T(8,128)(2,1)} %bitcast.13, s32[64,128,128]{2,1,0:T(8,128)} %bitcast.10, ...), custom_call_target="tpu_custom_call" | custom-call | tf_op jit(solution)/shard_map/layer/pallas_call | solution.py:374
  53.9 0.0 copy-start
  53.9 3.2 %copy.13 = bf16[1,1,64,128,128]{4,3,2,1,0:T(8,128)(2,1)} copy(bf16[1,1,64,128,128]{4,3,2,1,0:T(8,128)(2,1)} %bitcast.12) | data formatting | bytes 4194304
  57.1 0.0 copy-done
  57.1 0.7 %copy.14 = bf16[512,128]{1,0:T(8,128)(2,1)} copy(bf16[512,128]{1,0:T(8,128)(2,1)S(1)} %bitcast.14) | data formatting | bytes 262144
Async XLA Ops:
  53.9 3.2 %copy-start = (bf16[4,128,128]{2,1,0:T(8,128)(2,1)S(1)}, bf16[4,128,128]{2,1,0:T(8,128)(2,1)}, u32[]{:S(2)}) copy-start(bf16[4,128,128]{2,1,0:T(8,128)(2,1)} %get-tuple-element.5) | copy-start | bytes 393220

commit v3 on v2

--- a/solution.py
+++ b/solution.py
@@ -28,7 +28,6 @@
     wts,
     adj,
     sums,
-    edge_out,
     stage,
     merged,
     relayed,
@@ -36,7 +35,6 @@
     chain_v,
     chain,
     load_sem,
-    out_sem,
     h_send,
     h_recv,
     x_send,
@@ -128,19 +126,19 @@
         x_copy(block, part, n, to_core, 0, sem).wait_recv()
 
     put(c, 0, to_y)
-    put(c, 0, to_z[1])
-    put(c, 0, to_z[-1])
-    put(c, 1, to_z[1])
-    put(c, 1, to_z[-1])
-    put(c, 1, to_y)
+    for half in (1, 0):
+        for sign in (1, -1):
+            put(c, half, to_z[sign])
+        if half:
+            put(c, half, to_y)
+    put(c, 1, to_core)
     put(c, 0, to_core)
-    put(c, 1, to_core)
     loads[0].wait()
     x_put(r, 0, 4, to_row[0, 1], 1)
     x_put(r, 0, 4, to_row[0, -1], 2)
     x_put(r, 0, 4, to_row[1, 0], 0)
 
-    cols = table_v[1:2, :]
+    cols = table_v[1]
     wide = jnp.broadcast_to(cols, (slots, slots))
     at_s = lax.broadcasted_iota(jnp.int32, (slots, slots), 0)
     at_q = lax.broadcasted_iota(jnp.int32, (slots, slots), 1)
@@ -157,7 +155,7 @@
 
     def prepare(first, n):
         def one(t, carry):
-            keep = mask[t] * table[2, t] != 0
+            keep = mask[t] * table[2, 0, t] != 0
             kept = jnp.where(keep, wts[t].astype(F32), 0.0)
             adj[t] = kept.T.astype(BF16)
             return carry
@@ -173,20 +171,21 @@
 
     done = 8
     for s in range(1, 4):
+        near = {sign: col_of(yl, z - sign * s, k) for sign in (1, -1)}
+        far = {sign: col_of(1 - yl, z - sign * s, k) for sign in (1, -1)}
+        for half in (1, 0):
+            for sign in (1, -1):
+                got(near[sign], half)
+                if s < 3 or half == (0 if sign > 0 else 1):
+                    put(near[sign], half, to_z[sign])
+                if half:
+                    put(near[sign], half, to_y)
+                put(near[sign], half, to_core)
         for sign in (1, -1):
-            near = col_of(yl, z - sign * s, k)
-            far = col_of(1 - yl, z - sign * s, k)
-            for half in (0, 1):
-                got(near, half)
-                if s < 3 or half == (0 if sign > 0 else 1):
-                    put(near, half, to_z[sign])
-                if half:
-                    put(near, half, to_y)
-                put(near, half, to_core)
-            got(far, 0)
+            got(far[sign], 0)
             if s < 3:
-                put(far, 0, to_z[sign])
-            put(far, 0, to_core)
+                put(far[sign], 0, to_z[sign])
+            put(far[sign], 0, to_core)
         if s == 3:
             way = 1 - 2 * k
             put(col_of(1 - yl, z - 3 * way, k), 0, (r, col_of(yl, z + way, k)))
@@ -238,11 +237,11 @@
 
     def add(t, carry):
         before = chain[0, t]
-        part = jnp.dot(adj[t], hbuf[table[0, t]], preferred_element_type=F32)
+        part = jnp.dot(adj[t], hbuf[table[0, 0, t]], preferred_element_type=F32)
         sums[t] = part + jnp.where(before >= 0, sums[jnp.maximum(before, 0)], 0.0)
         return carry
 
-    lax.fori_loop(0, slots, add, 0, unroll=4)
+    lax.fori_loop(0, slots, add, 0, unroll=16)
 
     def total(block):
         final = chain[1, block]
@@ -326,22 +325,17 @@
     x_got(far_x, 0, 2, 7)
     x_got(far_x, 2, 2, 8)
 
-    def chunk_out(i):
-        part = pl.ds(i * CHUNK, CHUNK)
-        return pltpu.make_async_copy(edge_out.at[part], edge_grad.at[part], out_sem.at[i])
-
     def chunk(i, carry):
         for j in range(CHUNK):
             t = i * CHUNK + j
-            keep = mask[t] * table[2, t] != 0
+            keep = mask[t] * table[2, 0, t] != 0
             scores = lax.dot_general(
-                hbuf[table[0, t]],
-                xbuf[table[1, t]],
+                hbuf[table[0, 0, t]],
+                xbuf[table[1, 0, t]],
                 (((1,), (1,)), ((), ())),
                 preferred_element_type=F32,
             )
-            edge_out[t] = jnp.where(keep, scores, 0.0).astype(BF16)
-        chunk_out(i).start()
+            edge_grad[t] = jnp.where(keep, scores, 0.0).astype(BF16)
         return carry
 
     lax.fori_loop(0, slots // CHUNK, chunk, 0)
@@ -358,14 +352,12 @@
 
     for copy in started + x_started + g_started:
         copy.wait_send()
-    for i in range(slots // CHUNK):
-        chunk_out(i).wait()
 
 
 def local(features, weight, out_grad, tile_index, edge_mask, edge_weight):
     nodes, width = features.shape
     slots = edge_mask.shape[2]
-    table = tile_index[0, 0].T
+    table = tile_index[0].transpose(2, 0, 1)
     blocks = nodes // BLOCK
     vmem = pl.BlockSpec(memory_space=pltpu.VMEM)
     hbm = pl.BlockSpec(memory_space=pl.ANY)
@@ -374,10 +366,10 @@
     edge_grad, feature_grad = pl.pallas_call(
         kernel,
         in_specs=[pl.BlockSpec(memory_space=pltpu.SMEM), vmem, vmem, vmem, hbm, hbm, hbm],
-        out_specs=[hbm, vmem],
+        out_specs=[vmem, vmem],
         out_shape=[
-            jax.ShapeDtypeStruct((slots, *tile), BF16),
-            jax.ShapeDtypeStruct((blocks, *tile), BF16),
+            pltpu.VMEM((slots, *tile), BF16),
+            pltpu.VMEM((blocks, *tile), BF16),
         ],
         scratch_shapes=[
             pltpu.VMEM((4 * blocks * NZ, *tile), BF16),
@@ -386,7 +378,6 @@
             pltpu.VMEM((slots, *tile), BF16),
             pltpu.VMEM((slots, *tile), BF16),
             pltpu.VMEM((slots, *tile), F32),
-            pltpu.VMEM((slots, *tile), BF16),
             pltpu.VMEM((2 * blocks * NX, *tile), BF16),
             pltpu.VMEM((8, *tile), BF16),
             pltpu.VMEM((8, *tile), BF16),
@@ -394,7 +385,6 @@
             pltpu.VMEM((8, 128), jnp.int32),
             pltpu.SMEM((8, 128), jnp.int32),
             dma((4,)),
-            dma((slots // CHUNK,)),
             dma((62,)),
             dma((64,)),
             dma((9,)),

time: 57.9 us -> 50.1 us (0.87)
  Pallas kernels: 52 us -> 47.4 us
  local copies, waits for them, and re-layouts: 5.11 us -> 1.98 us
    pallas_call x1, Pallas kernels: 52 us -> 47.4 us  [local(): pl.pallas_call(kernel, in_specs=[pl.BlockSpec(memory_space=pltpu.SMEM), v...]
    unnamed x5 -> x2, local copies, waits for them, and re-layouts: 5.11 us -> 1.98 us
where the time goes in v3:
time: 50.1 us; the launch traced here: 50 us
  Pallas kernels  47.4 us (95%)
  local copies, waits for them, and re-layouts  1.98 us (4%)
  between operations  0.64 us (1%)
    pallas_call x1, Pallas kernels, local(): pl.pallas_call(kernel, in_specs=[pl.BlockSpec(memory_space=pltpu.SMEM), v...  47.4 us
    unnamed x2, local copies, waits for them, and re-layouts  1.98 us

profile of v3, /device:TPU:1, one launch (start us, length us, event | category | flops | bytes accessed | tf_op | source)
XLA Modules:
  0.0 50.0 jit_solution(13909807086367417736)
XLA Ops:
  0.6 47.4 %layer.1 = (bf16[64,128,128]{2,1,0:T(8,128)(2,1)S(1)}, bf16[4,128,128]{2,1,0:T(8,128)(2,1)S(1)}) custom-call(s32[3,1,64]{2,1,0:T(1,128)} %bitcast.13, s32[3,1,64]{2,1,0:T(1,128)} %bitcast.14, bf16[512,256]{1,0:T(8,128)(2,1)} %out_grad.1, bf16[128,256]{1,0:T(8,128)(2,1)} %weight.1, bf16[4,128,128]{2,1,0:T(8,128)(2,1)} %bitcast.12, s32[64,128,128]{2,1,0:T(8,128)} %bitcast.10, ...), custom_call_target="tpu_custom_call" | custom-call | tf_op jit(solution)/shard_map/layer/pallas_call | solution.py:366
  48.0 1.3 %copy.10 = bf16[1,1,64,128,128]{4,3,2,1,0:T(8,128)(2,1)} copy(bf16[1,1,64,128,128]{4,3,2,1,0:T(8,128)(2,1)S(1)} %bitcast.8) | data formatting | bytes 4194304
  49.4 0.7 %copy.11 = bf16[512,128]{1,0:T(8,128)(2,1)} copy(bf16[512,128]{1,0:T(8,128)(2,1)S(1)} %bitcast.9) | data formatting | bytes 262144

commit v4 on v3

v4 whole, which is shorter than its diff:
```python
import jax
import jax.numpy as jnp
from jax import lax
from jax.experimental import pallas as pl
from jax.experimental.pallas import tpu as pltpu
from jax.sharding import PartitionSpec as P

MESH = pl.DeviceIdType.MESH
BLOCK = 128
NX, NZ = 4, 8
CHUNK, GROUP = 8, 16
F32, BF16 = jnp.float32, jnp.bfloat16
RIDE, POST = (0, 1), (2, 3)


def kernel(
    table,
    table_v,
    out_grad,
    weight,
    features,
    edge_mask,
    edge_weight,
    edge_grad,
    feature_grad,
    hbuf,
    xbuf,
    mask,
    wts,
    adj,
    sums,
    stage,
    merged,
    relayed,
    landed,
    order_v,
    order,
    load_sem,
    h_send,
    h_recv,
    x_send,
    x_recv,
    g_send,
    g_recv,
):
    slots = mask.shape[0]
    r, c = lax.axis_index("row"), lax.axis_index("col")
    yh, x = r // NX, r % NX
    yl, z, k = c // (2 * NZ), (c // 2) % NZ, c % 2

    def col_of(yl, z, k):
        return (yl * NZ + (z + NZ) % NZ) * 2 + k

    def row_of(yh, x):
        return yh * NX + (x + NX) % NX

    to_z = {s: (r, col_of(yl, z + s, k)) for s in (1, -1)}
    to_y = (r, col_of(1 - yl, z, k))
    to_core = (r, col_of(yl, z, 1 - k))
    to_row = {
        (q, s): (row_of((yh + q) % 2, x + s), c)
        for q in (0, 1)
        for s in (-1, 0, 1)
        if q or s
    }

    loads = [
        pltpu.make_async_copy(src, dst, load_sem.at[i])
        for i, (src, dst) in enumerate(
            ((features, xbuf.at[pl.ds(4 * r, 4)]), (edge_mask, mask), (edge_weight, wts))
        )
    ]
    for load in loads:
        load.start()

    barrier = pltpu.get_barrier_semaphore()
    peers = [to_z[1], to_z[-1], to_y, to_core, *to_row.values()]
    for peer in peers:
        pl.semaphore_signal(barrier, inc=1, device_id=peer, device_id_type=MESH)

    folded = lax.dot_general(
        out_grad[...], weight[...], (((1,), (1,)), ((), ())), preferred_element_type=F32
    ).astype(BF16)
    for b in range(4):
        hbuf[4 * c + b] = folded[b * BLOCK : (b + 1) * BLOCK]
    pl.semaphore_wait(barrier, len(peers))

    def remote(src, dst, send_sem, recv_sem, device):
        return pltpu.make_async_remote_copy(
            src_ref=src,
            dst_ref=dst,
            send_sem=send_sem,
            recv_sem=recv_sem,
            device_id=device,
            device_id_type=MESH,
        )

    names = [("mate", b) for b in RIDE]
    names += [("near", s, sign, b) for s in (1, 2, 3) for sign in (1, -1) for b in (*POST, *RIDE)]
    names += [("near", 4, 1, b) for b in (*POST, *RIDE)]
    names += [("far", s, sign, b) for s in (1, 2, 3) for sign in (1, -1) for b in RIDE]
    names += [("far", 4, 1, b) for b in RIDE]
    names += [("late", s) for s in (0, 1, -1, 2, -2, 3, -3, 4)]
    names += [("core",)]
    h_sem = {name: i for i, name in enumerate(names)}

    sent = []

    def put(block, first, n, device, *name):
        piece = hbuf.at[pl.ds(4 * block + first, n)]
        remote(piece, piece, h_send.at[0], h_recv.at[h_sem[name]], device).start()
        sent.append(n)

    def got(block, first, n, *name):
        piece = hbuf.at[pl.ds(4 * block + first, n)]
        remote(piece, piece, h_send.at[0], h_recv.at[h_sem[name]], to_core).wait_recv()

    def put_core(block):
        put(block, 0, 4, to_core, "core")

    def x_put(block, first, n, device, sem):
        piece = xbuf.at[pl.ds(4 * block + first, n)]
        remote(piece, piece, x_send.at[0], x_recv.at[sem], device).start()

    def x_got(block, first, n, sem):
        piece = xbuf.at[pl.ds(4 * block + first, n)]
        remote(piece, piece, x_send.at[0], x_recv.at[sem], to_core).wait_recv()

    for b in RIDE:
        put(c, b, 1, to_y, "mate", b)
    for b in (*POST, *RIDE):
        for sign in (1, -1):
            put(c, b, 1, to_z[sign], "near", 1, sign, b)
    for b in POST:
        put(c, b, 1, to_y, "late", 0)
    put_core(c)
    loads[0].wait()
    x_put(r, 0, 4, to_row[0, 1], 1)
    x_put(r, 0, 4, to_row[0, -1], 2)

    square = (slots, slots)
    at_s = lax.broadcasted_iota(jnp.int32, square, 0)
    at_q = lax.broadcasted_iota(jnp.int32, square, 1)

    def upright(line):
        return jnp.sum(
            jnp.where(at_s == at_q, jnp.broadcast_to(line, square), 0), axis=1, keepdims=True
        )

    def gather(where, column):
        return jnp.sum(jnp.where(where, column, 0), axis=0, keepdims=True)

    cols = jnp.broadcast_to(table_v[1], square)
    col_up, row_up = upright(table_v[1]), upright(table_v[0])
    before = cols * slots + at_q < col_up * slots + at_s
    rank = jnp.sum(jnp.where(before, 1, 0), axis=1, keepdims=True)
    here = rank == at_q
    col_here = gather(here, col_up)
    col_before = gather(rank == at_q - 1, col_up)
    first_lane = at_q[0:1] == 0
    order_v[0:1, 0:slots] = gather(here, at_s)
    order_v[1:2, 0:slots] = gather(here, row_up)
    order_v[2:3, 0:slots] = jnp.where((col_here == col_before) & ~first_lane, 1, 0)
    order_v[3:4, 0:slots] = jnp.where(
        gather(col_up == at_q, 1) > 0, gather(col_up <= at_q, 1) - 1, -1
    )
    to_scalar = pltpu.make_async_copy(order_v, order, load_sem.at[3])
    to_scalar.start()
    mate = col_of(1 - yl, z, k)
    for b in RIDE:
        got(mate, b, 1, "mate", b)
        for sign in (1, -1):
            put(mate, b, 1, to_z[sign], "far", 1, sign, b)
    to_scalar.wait()
    loads[1].wait()
    loads[2].wait()

    def prepare(first, n):
        def one(i, carry):
            t = order[0, i]
            keep = mask[t] * table[2, 0, t] != 0
            kept = jnp.where(keep, wts[t].astype(F32), 0.0)
            adj[i] = kept.T.astype(BF16)
            return carry

        lax.fori_loop(first, first + n, one, 0, unroll=2)

    def late(s):
        block = col_of(1 - yl, z + s, k)
        got(block, 2, 2, "late", s)
        put_core(block)

    prepare(0, 8)
    done = 8
    for s in (1, 2, 3):
        near = {sign: col_of(yl, z - sign * s, k) for sign in (1, -1)}
        far = {sign: col_of(1 - yl, z - sign * s, k) for sign in (1, -1)}
        for b in (*POST, *RIDE):
            for sign in (1, -1):
                got(near[sign], b, 1, "near", s, sign, b)
                if s < 3:
                    put(near[sign], b, 1, to_z[sign], "near", s + 1, sign, b)
                elif b in (RIDE if sign > 0 else POST):
                    put(near[sign], b, 1, to_z[sign], "near", 4, 1, b)
                if b in POST:
                    put(near[sign], b, 1, to_y, "late", -sign * s)
        for sign in (1, -1):
            put_core(near[sign])
        for b in RIDE:
            for sign in (1, -1):
                got(far[sign], b, 1, "far", s, sign, b)
                if s < 3:
                    put(far[sign], b, 1, to_z[sign], "far", s + 1, sign, b)
            if s == 3:
                way = 1 - 2 * k
                put(
                    col_of(1 - yl, z - 3 * way, k),
                    b,
                    1,
                    (r, col_of(yl, z + way, k)),
                    "far",
                    4,
                    1,
                    b,
                )
        for back in (s - 1,) if s == 1 else (s - 1, 1 - s):
            late(back)
        if s == 1:
            x_put(r, 0, 4, to_row[1, 0], 0)
        if s == 2:
            left, right = row_of(yh, x - 1), row_of(yh, x + 1)
            x_got(left, 0, 4, 1)
            x_put(left, 0, 2, to_row[0, 1], 5)
            x_got(right, 0, 4, 2)
            x_put(right, 2, 2, to_row[0, -1], 5)
        if s == 3:
            other = row_of(1 - yh, x)
            x_got(other, 0, 4, 0)
            x_put(other, 0, 4, to_row[0, 1], 3)
            x_put(other, 0, 4, to_row[0, -1], 4)
        more = 24 if s < 3 else slots - done
        if more:
            prepare(done, more)
        done += more
    near, far = col_of(yl, z + 4, k), col_of(1 - yl, z + 4, k)
    for b in POST:
        got(near, b, 1, "near", 4, 1, b)
        put(near, b, 1, to_y, "late", 4)
    for b in RIDE:
        got(near, b, 1, "near", 4, 1, b)
    put_core(near)
    for b in RIDE:
        got(far, b, 1, "far", 4, 1, b)
    for s in (3, -3, 4):
        late(s)
    left, right = row_of(1 - yh, x - 1), row_of(1 - yh, x + 1)
    x_got(left, 0, 4, 3)
    x_put(left, 0, 2, to_row[0, 1], 5)
    x_got(right, 0, 4, 4)
    x_put(right, 2, 2, to_row[0, -1], 5)
    got(0, 0, 8 * NZ, "core")

    def group(g, carry):
        run = sums[g * GROUP]
        for j in range(GROUP):
            i = g * GROUP + j
            added = jnp.dot(adj[i], hbuf[order[1, i]], preferred_element_type=F32)
            run = added + jnp.where(order[2, i] != 0, run, 0.0)
            sums[i + 1] = run
        return carry

    sums[0] = jnp.zeros((BLOCK, BLOCK), F32)
    lax.fori_loop(0, slots // GROUP, group, 0)

    def total(block):
        at = order[3, block]
        return jnp.where(at >= 0, sums[at + 1], 0.0)

    def fill(dest):
        for b in range(4):
            stage[4 * dest + b] = total(4 * dest + b).astype(BF16)

    def g_put(src, dst, sem, device):
        remote(src, dst, g_send.at[0 if sem < 4 else 1], g_recv.at[sem], device).start()

    def edges(first, n):
        def chunk(i, carry):
            for j in range(CHUNK):
                t = i * CHUNK + j
                keep = mask[t] * table[2, 0, t] != 0
                scores = lax.dot_general(
                    hbuf[table[0, 0, t]],
                    xbuf[table[1, 0, t]],
                    (((1,), (1,)), ((), ())),
                    preferred_element_type=F32,
                )
                edge_grad[t] = jnp.where(keep, scores, 0.0).astype(BF16)
            return carry

        lax.fori_loop(first // CHUNK, (first + n) // CHUNK, chunk, 0)

    sides = ((1, 0), (-1, 1))
    for q in (1, 0):
        dest = row_of((yh + q) % 2, x + 2)
        fill(dest)
        for s, half in sides:
            i = 2 * q + half
            g_put(
                stage.at[pl.ds(4 * dest + 2 * half, 2)],
                relayed.at[pl.ds(2 * i, 2)],
                i,
                to_row[0, s],
            )
    dest = row_of(1 - yh, x)
    fill(dest)
    g_put(stage.at[pl.ds(4 * dest, 4)], landed.at[pl.ds(16, 4)], 4, to_row[1, 0])
    for q in (1, 0):
        for s, half in sides:
            fill(row_of((yh + q) % 2, x + s))
    x_got(0, 0, 8, 5)
    edges(0, slots // 4)
    part = stage.at[pl.ds(0, 8)]
    remote(part, part, g_send.at[0], g_recv.at[0], to_core).wait_send()
    for q in (1, 0):
        for s, half in sides:
            dest = row_of((yh + q) % 2, x + s)
            i = 2 * q + half
            plain = 1 - half
            g_put(
                stage.at[pl.ds(4 * dest + 2 * plain, 2)],
                landed.at[pl.ds(4 * i + 2 * plain, 2)],
                4,
                to_row[q, s],
            )
    edges(slots // 4, slots // 4)
    for q in (1, 0):
        for s, half in sides:
            dest = row_of((yh + q) % 2, x + s)
            i = 2 * q + half
            into = relayed.at[pl.ds(2 * i, 2)]
            remote(into, into, g_send.at[0], g_recv.at[i], to_core).wait_recv()
            for b in (0, 1):
                merged[2 * i + b] = (
                    total(4 * dest + 2 * half + b) + relayed[2 * i + b].astype(F32)
                ).astype(BF16)
            g_put(
                merged.at[pl.ds(2 * i, 2)],
                landed.at[pl.ds(4 * i + 2 * half, 2)],
                4,
                to_row[q, s],
            )
    edges(slots // 2, slots // 2)
    remote(landed, landed, g_send.at[0], g_recv.at[4], to_core).wait_recv()
    for b in range(4):
        value = total(4 * r + b)
        for i in range(5):
            value += landed[4 * i + b].astype(F32)
        feature_grad[b] = value.astype(BF16)

    part = hbuf.at[pl.ds(0, sum(sent))]
    remote(part, part, h_send.at[0], h_recv.at[0], to_core).wait_send()
    part = xbuf.at[pl.ds(0, 28)]
    remote(part, part, x_send.at[0], x_recv.at[0], to_core).wait_send()
    remote(landed, landed, g_send.at[1], g_recv.at[0], to_core).wait_send()


def local(features, weight, out_grad, tile_index, edge_mask, edge_weight):
    nodes, width = features.shape
    slots = edge_mask.shape[2]
    table = tile_index[0].transpose(2, 0, 1)
    blocks = nodes // BLOCK
    rows, cols = 4 * 4 * NZ, 4 * 2 * NX
    vmem = pl.BlockSpec(memory_space=pltpu.VMEM)
    hbm = pl.BlockSpec(memory_space=pl.ANY)
    dma = pltpu.SemaphoreType.DMA
    tile = (BLOCK, BLOCK)

    edge_grad, feature_grad = pl.pallas_call(
        kernel,
        in_specs=[pl.BlockSpec(memory_space=pltpu.SMEM), vmem, vmem, vmem, hbm, hbm, hbm],
        out_specs=[vmem, vmem],
        out_shape=[pltpu.VMEM((slots, *tile), BF16), pltpu.VMEM((blocks, *tile), BF16)],
        scratch_shapes=[
            pltpu.VMEM((rows, *tile), BF16),
            pltpu.VMEM((cols, *tile), BF16),
            pltpu.VMEM((slots, *tile), jnp.int32),
            pltpu.VMEM((slots, *tile), BF16),
            pltpu.VMEM((slots, *tile), BF16),
            pltpu.VMEM((slots + 1, *tile), F32),
            pltpu.VMEM((cols, *tile), BF16),
            pltpu.VMEM((8, *tile), BF16),
            pltpu.VMEM((8, *tile), BF16),
            pltpu.VMEM((20, *tile), BF16),
            pltpu.VMEM((8, 128), jnp.int32),
            pltpu.SMEM((8, 128), jnp.int32),
            dma((4,)),
            dma((1,)),
            dma((53,)),
            dma((1,)),
            dma((6,)),
            dma((2,)),
            dma((5,)),
        ],
        compiler_params=pltpu.CompilerParams(
            collective_id=0, has_side_effects=True, vmem_limit_bytes=56 << 20
        ),
        name="layer",
    )(
        table,
        table,
        out_grad,
        weight,
        features.reshape(blocks, *tile),
        edge_mask[0, 0],
        edge_weight[0, 0],
    )
    return (edge_grad[None, None], feature_grad.reshape(nodes, width))


def solution(mesh):
    in_specs = (
        P(("col", "row"), None),
        P(),
        P(("row", "col"), None),
        P("row", "col", None, None),
        P("row", "col", None, None, None),
        P("row", "col", None, None, None),
    )
    out_specs = (P("row", "col", None, None, None), P(("col", "row"), None))
    return jax.shard_map(local, mesh=mesh, in_specs=in_specs, out_specs=out_specs, check_vma=False)
```

time: 50.1 us -> 47.5 us (0.948)
  Pallas kernels: 47.4 us -> 44.7 us
    pallas_call x1, Pallas kernels: 47.4 us -> 44.7 us  [local(): pl.pallas_call(kernel, in_specs=[pl.BlockSpec(memory_space=pltpu.SMEM), v...]
where the time goes in v4:
time: 47.5 us; the launch traced here: 47.4 us
  Pallas kernels  44.7 us (94%)
  local copies, waits for them, and re-layouts  1.98 us (4%)
  between operations  0.64 us (1%)
    pallas_call x1, Pallas kernels, local(): pl.pallas_call(kernel, in_specs=[pl.BlockSpec(memory_space=pltpu.SMEM), v...  44.7 us
    unnamed x2, local copies, waits for them, and re-layouts  1.98 us

profile of v4, /device:TPU:1, one launch (start us, length us, event | category | flops | bytes accessed | tf_op | source)
XLA Modules:
  0.0 47.4 jit_solution(2941098920226198286)
XLA Ops:
  0.6 44.7 %layer.1 = (bf16[64,128,128]{2,1,0:T(8,128)(2,1)S(1)}, bf16[4,128,128]{2,1,0:T(8,128)(2,1)S(1)}) custom-call(s32[3,1,64]{2,1,0:T(1,128)} %bitcast.13, s32[3,1,64]{2,1,0:T(1,128)} %bitcast.14, bf16[512,256]{1,0:T(8,128)(2,1)} %out_grad.1, bf16[128,256]{1,0:T(8,128)(2,1)} %weight.1, bf16[4,128,128]{2,1,0:T(8,128)(2,1)} %bitcast.12, s32[64,128,128]{2,1,0:T(8,128)} %bitcast.10, ...), custom_call_target="tpu_custom_call" | custom-call | tf_op jit(solution)/shard_map/layer/pallas_call | solution.py:378
  45.4 1.3 %copy.10 = bf16[1,1,64,128,128]{4,3,2,1,0:T(8,128)(2,1)} copy(bf16[1,1,64,128,128]{4,3,2,1,0:T(8,128)(2,1)S(1)} %bitcast.8) | data formatting | bytes 4194304
  46.7 0.7 %copy.11 = bf16[512,128]{1,0:T(8,128)(2,1)} copy(bf16[512,128]{1,0:T(8,128)(2,1)S(1)} %bitcast.9) | data formatting | bytes 262144

commit v5 on v4

--- a/solution.py
+++ b/solution.py
@@ -8,7 +8,7 @@
 MESH = pl.DeviceIdType.MESH
 BLOCK = 128
 NX, NZ = 4, 8
-CHUNK, GROUP = 8, 16
+CHUNK, GROUP = 8, 32
 F32, BF16 = jnp.float32, jnp.bfloat16
 RIDE, POST = (0, 1), (2, 3)
 
@@ -96,8 +96,8 @@
         )
 
     names = [("mate", b) for b in RIDE]
-    names += [("near", s, sign, b) for s in (1, 2, 3) for sign in (1, -1) for b in (*POST, *RIDE)]
-    names += [("near", 4, 1, b) for b in (*POST, *RIDE)]
+    names += [("near", s, sign, b) for s in (1, 2, 3) for sign in (1, -1) for b in (*RIDE, *POST)]
+    names += [("near", 4, 1, b) for b in (*RIDE, *POST)]
     names += [("far", s, sign, b) for s in (1, 2, 3) for sign in (1, -1) for b in RIDE]
     names += [("far", 4, 1, b) for b in RIDE]
     names += [("late", s) for s in (0, 1, -1, 2, -2, 3, -3, 4)]
@@ -128,7 +128,7 @@
 
     for b in RIDE:
         put(c, b, 1, to_y, "mate", b)
-    for b in (*POST, *RIDE):
+    for b in (*RIDE, *POST):
         for sign in (1, -1):
             put(c, b, 1, to_z[sign], "near", 1, sign, b)
     for b in POST:
@@ -187,7 +187,7 @@
 
     def late(s):
         block = col_of(1 - yl, z + s, k)
-        got(block, 2, 2, "late", s)
+        got(block, POST[0], len(POST), "late", s)
         put_core(block)
 
     prepare(0, 8)
@@ -195,12 +195,12 @@
     for s in (1, 2, 3):
         near = {sign: col_of(yl, z - sign * s, k) for sign in (1, -1)}
         far = {sign: col_of(1 - yl, z - sign * s, k) for sign in (1, -1)}
-        for b in (*POST, *RIDE):
+        for b in (*RIDE, *POST):
             for sign in (1, -1):
                 got(near[sign], b, 1, "near", s, sign, b)
                 if s < 3:
                     put(near[sign], b, 1, to_z[sign], "near", s + 1, sign, b)
-                elif b in (RIDE if sign > 0 else POST):
+                elif b in ((0, 1) if sign > 0 else (2, 3)):
                     put(near[sign], b, 1, to_z[sign], "near", 4, 1, b)
                 if b in POST:
                     put(near[sign], b, 1, to_y, "late", -sign * s)
@@ -281,7 +281,7 @@
             stage[4 * dest + b] = total(4 * dest + b).astype(BF16)
 
     def g_put(src, dst, sem, device):
-        remote(src, dst, g_send.at[0 if sem < 4 else 1], g_recv.at[sem], device).start()
+        remote(src, dst, g_send.at[0 if sem < 8 else 1], g_recv.at[sem], device).start()
 
     def edges(first, n):
         def chunk(i, carry):
@@ -305,22 +305,21 @@
         fill(dest)
         for s, half in sides:
             i = 2 * q + half
-            g_put(
-                stage.at[pl.ds(4 * dest + 2 * half, 2)],
-                relayed.at[pl.ds(2 * i, 2)],
-                i,
-                to_row[0, s],
-            )
+            for p in (0, 1):
+                g_put(
+                    stage.at[pl.ds(4 * dest + 2 * half + p, 1)],
+                    relayed.at[pl.ds(2 * i + p, 1)],
+                    2 * i + p,
+                    to_row[0, s],
+                )
     dest = row_of(1 - yh, x)
     fill(dest)
-    g_put(stage.at[pl.ds(4 * dest, 4)], landed.at[pl.ds(16, 4)], 4, to_row[1, 0])
+    g_put(stage.at[pl.ds(4 * dest, 4)], landed.at[pl.ds(16, 4)], 8, to_row[1, 0])
     for q in (1, 0):
         for s, half in sides:
             fill(row_of((yh + q) % 2, x + s))
     x_got(0, 0, 8, 5)
     edges(0, slots // 4)
-    part = stage.at[pl.ds(0, 8)]
-    remote(part, part, g_send.at[0], g_recv.at[0], to_core).wait_send()
     for q in (1, 0):
         for s, half in sides:
             dest = row_of((yh + q) % 2, x + s)
@@ -329,7 +328,7 @@
             g_put(
                 stage.at[pl.ds(4 * dest + 2 * plain, 2)],
                 landed.at[pl.ds(4 * i + 2 * plain, 2)],
-                4,
+                8,
                 to_row[q, s],
             )
     edges(slots // 4, slots // 4)
@@ -337,20 +336,20 @@
         for s, half in sides:
             dest = row_of((yh + q) % 2, x + s)
             i = 2 * q + half
-            into = relayed.at[pl.ds(2 * i, 2)]
-            remote(into, into, g_send.at[0], g_recv.at[i], to_core).wait_recv()
-            for b in (0, 1):
-                merged[2 * i + b] = (
-                    total(4 * dest + 2 * half + b) + relayed[2 * i + b].astype(F32)
+            for p in (0, 1):
+                into = relayed.at[pl.ds(2 * i + p, 1)]
+                remote(into, into, g_send.at[0], g_recv.at[2 * i + p], to_core).wait_recv()
+                merged[2 * i + p] = (
+                    total(4 * dest + 2 * half + p) + relayed[2 * i + p].astype(F32)
                 ).astype(BF16)
-            g_put(
-                merged.at[pl.ds(2 * i, 2)],
-                landed.at[pl.ds(4 * i + 2 * half, 2)],
-                4,
-                to_row[q, s],
-            )
+                g_put(
+                    merged.at[pl.ds(2 * i + p, 1)],
+                    landed.at[pl.ds(4 * i + 2 * half + p, 1)],
+                    8,
+                    to_row[q, s],
+                )
     edges(slots // 2, slots // 2)
-    remote(landed, landed, g_send.at[0], g_recv.at[4], to_core).wait_recv()
+    remote(landed, landed, g_send.at[0], g_recv.at[8], to_core).wait_recv()
     for b in range(4):
         value = total(4 * r + b)
         for i in range(5):
@@ -362,6 +361,19 @@
     part = xbuf.at[pl.ds(0, 28)]
     remote(part, part, x_send.at[0], x_recv.at[0], to_core).wait_send()
     remote(landed, landed, g_send.at[1], g_recv.at[0], to_core).wait_send()
+    part = stage.at[pl.ds(0, 8)]
+    remote(part, part, g_send.at[0], g_recv.at[0], to_core).wait_send()
+
+
+def write(edges, grads, edges_out, grads_out, sem):
+    copies = [
+        pltpu.make_async_copy(edges, edges_out, sem.at[0]),
+        pltpu.make_async_copy(grads, grads_out, sem.at[1]),
+    ]
+    for copy in copies:
+        copy.start()
+    for copy in copies:
+        copy.wait()
 
 
 def local(features, weight, out_grad, tile_index, edge_mask, edge_weight):
@@ -399,7 +411,7 @@
             dma((1,)),
             dma((6,)),
             dma((2,)),
-            dma((5,)),
+            dma((9,)),
         ],
         compiler_params=pltpu.CompilerParams(
             collective_id=0, has_side_effects=True, vmem_limit_bytes=56 << 20
@@ -414,6 +426,19 @@
         edge_mask[0, 0],
         edge_weight[0, 0],
     )
+    edge_grad = pltpu.with_memory_space_constraint(edge_grad, pltpu.VMEM)
+    feature_grad = pltpu.with_memory_space_constraint(feature_grad, pltpu.VMEM)
+    edge_grad, feature_grad = pl.pallas_call(
+        write,
+        in_specs=[vmem, vmem],
+        out_specs=[hbm, hbm],
+        out_shape=[
+            jax.ShapeDtypeStruct(edge_grad.shape, BF16),
+            jax.ShapeDtypeStruct(feature_grad.shape, BF16),
+        ],
+        scratch_shapes=[dma((2,))],
+        name="write",
+    )(edge_grad, feature_grad)
     return (edge_grad[None, None], feature_grad.reshape(nodes, width))
 
 

time: 47.5 us -> 46 us (0.968)
  local copies, waits for them, and re-layouts: 1.98 us -> 0 us
  Pallas kernels: 44.7 us -> 45.3 us
    unnamed x2 -> x0, local copies, waits for them, and re-layouts: 1.98 us -> none
    pallas_call x0 -> x1, Pallas kernels: none -> 1.36 us  [local(): pl.pallas_call(write, in_specs=[vmem, vmem], out_specs=[hbm, hbm], out_sh...]
    pallas_call x1, Pallas kernels: 44.7 us -> 43.9 us  [local(): pl.pallas_call(kernel, in_specs=[pl.BlockSpec(memory_space=pltpu.SMEM), v...]
where the time goes in v5:
time: 46 us; the launch traced here: 45.9 us
  Pallas kernels  45.3 us (98%)
  between operations  0.64 us (1%)
    pallas_call x1, Pallas kernels, local(): pl.pallas_call(kernel, in_specs=[pl.BlockSpec(memory_space=pltpu.SMEM), v...  43.9 us
    pallas_call x1, Pallas kernels, local(): pl.pallas_call(write, in_specs=[vmem, vmem], out_specs=[hbm, hbm], out_sh...  1.36 us

profile of v5, /device:TPU:1, one launch (start us, length us, event | category | flops | bytes accessed | tf_op | source)
XLA Modules:
  0.0 45.9 jit_solution(13121198988548106816)
XLA Ops:
  0.6 43.9 %layer.1 = (bf16[64,128,128]{2,1,0:T(8,128)(2,1)S(1)}, bf16[4,128,128]{2,1,0:T(8,128)(2,1)S(1)}) custom-call(s32[3,1,64]{2,1,0:T(1,128)} %bitcast.11, s32[3,1,64]{2,1,0:T(1,128)} %bitcast.12, bf16[512,256]{1,0:T(8,128)(2,1)} %out_grad.1, bf16[128,256]{1,0:T(8,128)(2,1)} %weight.1, bf16[4,128,128]{2,1,0:T(8,128)(2,1)} %bitcast.10, s32[64,128,128]{2,1,0:T(8,128)} %bitcast.8, ...), custom_call_target="tpu_custom_call" | custom-call | tf_op jit(solution)/shard_map/layer/pallas_call | solution.py:390
  44.6 1.4 %write.1 = (bf16[64,128,128]{2,1,0:T(8,128)(2,1)}, bf16[4,128,128]{2,1,0:T(8,128)(2,1)}) custom-call(bf16[64,128,128]{2,1,0:T(8,128)(2,1)S(1)} %get-tuple-element.6.edges, bf16[4,128,128]{2,1,0:T(8,128)(2,1)S(1)} %get-tuple-element.7.grads), custom_call_target="tpu_custom_call" | custom-call | tf_op jit(solution)/shard_map/write/pallas_call | solution.py:431

commit v6 on v5

--- a/solution.py
+++ b/solution.py
@@ -8,7 +8,7 @@
 MESH = pl.DeviceIdType.MESH
 BLOCK = 128
 NX, NZ = 4, 8
-CHUNK, GROUP = 8, 32
+CHUNK, GROUP = 8, 64
 F32, BF16 = jnp.float32, jnp.bfloat16
 RIDE, POST = (0, 1), (2, 3)
 

time: 46 us -> 45.9 us (level)
  no operation moved by 1% of the time
where the time goes in v6:
time: 45.9 us; the launch traced here: 45.8 us
  Pallas kernels  45.1 us (98%)
  between operations  0.64 us (1%)
    pallas_call x1, Pallas kernels, local(): pl.pallas_call(kernel, in_specs=[pl.BlockSpec(memory_space=pltpu.SMEM), v...  43.8 us
    pallas_call x1, Pallas kernels, local(): pl.pallas_call(write, in_specs=[vmem, vmem], out_specs=[hbm, hbm], out_sh...  1.36 us

profile of v6, /device:TPU:1, one launch (start us, length us, event | category | flops | bytes accessed | tf_op | source)
XLA Modules:
  0.0 45.8 jit_solution(15194611743558206062)
XLA Ops:
  0.6 43.8 %layer.1 = (bf16[64,128,128]{2,1,0:T(8,128)(2,1)S(1)}, bf16[4,128,128]{2,1,0:T(8,128)(2,1)S(1)}) custom-call(s32[3,1,64]{2,1,0:T(1,128)} %bitcast.11, s32[3,1,64]{2,1,0:T(1,128)} %bitcast.12, bf16[512,256]{1,0:T(8,128)(2,1)} %out_grad.1, bf16[128,256]{1,0:T(8,128)(2,1)} %weight.1, bf16[4,128,128]{2,1,0:T(8,128)(2,1)} %bitcast.10, s32[64,128,128]{2,1,0:T(8,128)} %bitcast.8, ...), custom_call_target="tpu_custom_call" | custom-call | tf_op jit(solution)/shard_map/layer/pallas_call | solution.py:390
  44.4 1.4 %write.1 = (bf16[64,128,128]{2,1,0:T(8,128)(2,1)}, bf16[4,128,128]{2,1,0:T(8,128)(2,1)}) custom-call(bf16[64,128,128]{2,1,0:T(8,128)(2,1)S(1)} %get-tuple-element.6.edges, bf16[4,128,128]{2,1,0:T(8,128)(2,1)S(1)} %get-tuple-element.7.grads), custom_call_target="tpu_custom_call" | custom-call | tf_op jit(solution)/shard_map/write/pallas_call | solution.py:431
